TPU v7x, 32 devices: a whole 2x2x4 slice. The times are simulated.
32 devices in a mesh: seq: 8 (over y, x, core), head: 4 (over z).
Axes of the slice: x: 2, y: 2, z: 4, core: 2. Of those that a mesh axis runs over, the one named last changes fastest.
Arguments:
- qk: bfloat16 [16384, 2048], P('seq', 'head'), may hold values from -480 to 480, as said below
- values: bfloat16 [16384, 2048], P('seq', 'head'), may hold values from -6 to 6
- bucket: int32 [64, 16], replicated, may hold values from 0 to 1
- pair_row: int32 [8, 8, 3], P('seq'), may hold values from 0 to 7, as said below
- pair_col: int32 [8, 8, 3], P('seq'), may hold values from 0 to 7, as said below
- pair_count: int32 [8, 8], P('seq'), may hold values from 0 to 3, as said below
- w_out: bfloat16 [2048, 2048], P('head'), may hold values from -0.125 to 0.125
Outputs:
- projected: bfloat16 [16384, 2048], P(('seq', 'head'))
Inputs may be any that keep to these rules, and one draw needn't show every extreme that they name: `pair_row`: every value is a local block index of the shard it refers to. `pair_col`: every value is a local block index; a pair never joins a block with itself. `pair_count`: some shard has 3 live slots towards every shard in every draw. `qk`: row scales of the vectors may differ widely.
All inputs are finite; a program needn't handle non-finite values.
Results may differ from a plain program's by a relative error of at most 0.014.
Values may be sent and summed in bfloat16 or wider, within the bound.
No kernel may reach another device: no remote copies, remote signals or barrier semaphores. Data moves between devices by JAX's collectives and lax.ppermute only.
A program may use at most 128 MiB of HBM per device.

v0:
```python
import math
import jax
import jax.numpy as jnp
from jax import lax
from jax.sharding import PartitionSpec as P

HD = 128
BLOCK = 256
NEG = -1e30


def inverse_norms(block):
    wide = block.astype(jnp.float32)
    return (lax.rsqrt(jnp.mean(wide * wide, axis=-1) + 1e-06) / math.sqrt(block.shape[-1])).T


def softmax_side(scores, axis):
    top = jnp.max(scores, axis=axis)
    weights = jnp.exp(scores - jnp.expand_dims(top, axis))
    total = jnp.sum(weights, axis=axis)
    return (top, total, weights.astype(jnp.bfloat16))


def pair_parts(q_a, v_a, q_b, v_b, keep):
    gram = jnp.einsum("shd,thd->hst", q_a, q_b, preferred_element_type=jnp.float32)
    srow = gram * inverse_norms(q_b)[:, None, :]
    scol = gram * inverse_norms(q_a)[:, :, None]
    mrow, lrow, prow = softmax_side(srow, 2)
    acc_row = jnp.einsum("hst,thd->shd", prow, v_b, preferred_element_type=jnp.float32)
    mcol, lcol, pcol = softmax_side(scol, 1)
    acc_col = jnp.einsum("hst,shd->thd", pcol, v_a, preferred_element_type=jnp.float32)
    mrow = jnp.where(keep[:, None], mrow, NEG)
    lrow = jnp.where(keep[:, None], lrow, 0.0)
    acc_row = jnp.where(keep[None, :, None], acc_row, 0.0)
    mcol = jnp.where(keep[:, None], mcol, NEG)
    lcol = jnp.where(keep[:, None], lcol, 0.0)
    acc_col = jnp.where(keep[None, :, None], acc_col, 0.0)
    return ((mrow, lrow, acc_row), (mcol, lcol, acc_col))


def diagonal_parts(q_a, v_a):
    gram = jnp.einsum("shd,thd->hst", q_a, q_a, preferred_element_type=jnp.float32)
    srow = gram * inverse_norms(q_a)[:, None, :]
    eye = jnp.arange(q_a.shape[0])[:, None] == jnp.arange(q_a.shape[0])[None, :]
    srow = jnp.where(eye[None], NEG, srow)
    mrow, lrow, prow = softmax_side(srow, 2)
    acc_row = jnp.einsum("hst,thd->shd", prow, v_a, preferred_element_type=jnp.float32)
    return (mrow, lrow, acc_row)


def group_parts(item):
    q_a, v_a, q_b, v_b, keep = item
    return jax.vmap(pair_parts)(q_a, v_a, q_b, v_b, keep)


def body(qk, values, bucket, pair_row, pair_col, pair_count, w_out):
    shards = lax.axis_size("seq")
    seq_dev, width = qk.shape
    heads_here = width // HD
    blocks_here = seq_dev // BLOCK
    slots = pair_row.shape[2]
    total_slots = shards * slots
    q_blocks = qk.reshape(blocks_here, BLOCK, heads_here, HD)
    v_blocks = values.reshape(blocks_here, BLOCK, heads_here, HD)
    wanted = lax.all_to_all(pair_col, "seq", split_axis=1, concat_axis=0, tiled=True).reshape(
        total_slots
    )
    sent_q = q_blocks[wanted].reshape(shards, slots, BLOCK, heads_here, HD)
    sent_v = v_blocks[wanted].reshape(shards, slots, BLOCK, heads_here, HD)
    got_q, got_v = (
        lax.all_to_all(sent_q, "seq", split_axis=0, concat_axis=0, tiled=True),
        lax.all_to_all(sent_v, "seq", split_axis=0, concat_axis=0, tiled=True),
    )
    row_index = pair_row.reshape(total_slots)
    seq_id = lax.axis_index("seq")
    head_id = lax.axis_index("head")
    my_buckets = lax.dynamic_slice_in_dim(bucket, head_id * heads_here, heads_here, 1)
    row_glob = seq_id * blocks_here + row_index
    owner = jnp.repeat(jnp.arange(shards, dtype=jnp.int32), slots)
    col_glob = owner * blocks_here + pair_col.reshape(total_slots)
    live = (jnp.arange(slots, dtype=jnp.int32)[None, :] < pair_count[0][:, None]).reshape(
        total_slots
    )
    keep = live[:, None] & (my_buckets[row_glob] == my_buckets[col_glob])
    mine_q = q_blocks[row_index].reshape(shards, slots, BLOCK, heads_here, HD)
    mine_v = v_blocks[row_index].reshape(shards, slots, BLOCK, heads_here, HD)
    row_side, col_side = lax.map(
        group_parts, (mine_q, mine_v, got_q, got_v, keep.reshape(shards, slots, heads_here))
    )
    back_m, back_l, back_acc = lax.all_to_all(
        col_side, "seq", split_axis=0, concat_axis=0, tiled=True
    )
    diag_m, diag_l, diag_acc = jax.vmap(diagonal_parts)(q_blocks, v_blocks)
    index_all = jnp.concatenate([row_index, wanted], axis=0)
    m_all = jnp.concatenate(
        [
            row_side[0].reshape(total_slots, heads_here, BLOCK),
            back_m.reshape(total_slots, heads_here, BLOCK),
        ],
        axis=0,
    )
    l_all = jnp.concatenate(
        [
            row_side[1].reshape(total_slots, heads_here, BLOCK),
            back_l.reshape(total_slots, heads_here, BLOCK),
        ],
        axis=0,
    )
    acc_all = jnp.concatenate(
        [
            row_side[2].reshape(total_slots, BLOCK, heads_here, HD),
            back_acc.reshape(total_slots, BLOCK, heads_here, HD),
        ],
        axis=0,
    )
    onehot = index_all[:, None] == jnp.arange(blocks_here, dtype=jnp.int32)[None, :]
    m_tot = jnp.maximum(
        diag_m, jnp.max(jnp.where(onehot[:, :, None, None], m_all[:, None], NEG), axis=0)
    )
    m_at = jnp.sum(jnp.where(onehot[:, :, None, None], m_tot[None], 0.0), axis=1)
    scale_all = jnp.exp(m_all - m_at)
    onehot_f = onehot.astype(jnp.float32)
    scale_diag = jnp.exp(diag_m - m_tot)
    l_tot = diag_l * scale_diag + jnp.einsum(
        "kb,khs->bhs", onehot_f, l_all * scale_all, precision=lax.Precision.HIGHEST
    )
    weighted = acc_all * jnp.transpose(scale_all, (0, 2, 1))[..., None]
    acc_tot = diag_acc * jnp.transpose(scale_diag, (0, 2, 1))[..., None]
    acc_tot = acc_tot + jnp.einsum(
        "kb,kshd->bshd", onehot_f, weighted, precision=lax.Precision.HIGHEST
    )
    attn = (
        (acc_tot / jnp.transpose(l_tot, (0, 2, 1))[..., None])
        .reshape(seq_dev, width)
        .astype(jnp.bfloat16)
    )
    mixed = lax.all_to_all(attn, "head", split_axis=0, concat_axis=1, tiled=True)
    summed = jnp.dot(
        mixed, lax.all_gather(w_out, "head", axis=0, tiled=True), preferred_element_type=jnp.float32
    )
    return summed.astype(jnp.bfloat16)


def solution(mesh):
    return jax.shard_map(
        body,
        mesh=mesh,
        in_specs=(
            P("seq", "head"),
            P("seq", "head"),
            P(),
            P("seq", None, None),
            P("seq", None, None),
            P("seq", None),
            P("head", None),
        ),
        out_specs=P(("seq", "head"), None),
        check_vma=False,
    )
```

profile of v0, /device:TPU:2, one launch (start us, length us, event | category | flops | bytes accessed | tf_op | source)
XLA Modules:
  0.0 551.1 jit_solution(3559827569345628649)
XLA Ops:
  7.9 4.3 all-to-all-start
  12.2 4.0 reshape.322
  18.3 4.4 gather_fusion.3
  22.7 4.7 all-to-all-start.1
  27.4 4.0 reshape.323
  31.4 3.4 copy.213
  34.8 5.9 %gather_fusion.4 = bf16[24,256,4,128]{3,1,2,0:T(8,128)(2,1)} fusion(bf16[8,256,4,128]{3,1,2,0:T(8,128)(2,1)} %copy.213, s32[1024]{0:T(1024)S(1)} %pad_clamp_fusion), kind=kCustom, calls=%fused_computation.4 | custom fusion | bytes 12583008 | tf_op jit(solution)/shard_map/gather | solution.py:69
  40.7 8.6 %copy.225 = bf16[8,3,256,4,128]{2,4,3,1,0:T(8,128)(2,1)} copy(bf16[8,3,256,4,128]{4,2,3,1,0:T(8,128)(2,1)} %bitcast.132) | data formatting | bytes 12582912 | tf_op jit(solution)/shard_map/reshape | solution.py:69
  49.3 48.2 %all-to-all-done.1 = bf16[8,3,256,4,128]{4,2,3,1,0:T(8,128)(2,1)} async-done(((bf16[8,3,256,4,128]{4,2,3,1,0:T(8,128)(2,1)}), bf16[8,3,256,4,128]{4,2,3,1,0:T(8,128)(2,1)}, u32[]{:S(2)}, u32[]{:S(2)}) %all-to-all-start.1) | async-done | bytes 6291488 | tf_op jit(solution)/shard_map/all_to_all | solution.py:71
  97.6 6.2 %all-to-all-start.2 = ((bf16[8,3,256,4,128]{2,4,3,1,0:T(8,128)(2,1)}), bf16[8,3,256,4,128]{2,4,3,1,0:T(8,128)(2,1)}, u32[]{:S(2)}, u32[]{:S(2)}) async-start(bf16[8,3,256,4,128]{2,4,3,1,0:T(8,128)(2,1)} %copy.225), calls=%async_computation.2 | async-start | bytes 12582912 | tf_op jit(solution)/shard_map/all_to_all | solution.py:72
  104.0 4.4 gather_fusion.2
  108.5 5.9 %gather_fusion.5 = bf16[24,256,4,128]{3,1,2,0:T(8,128)(2,1)} fusion(bf16[8,256,4,128]{3,1,2,0:T(8,128)(2,1)} %copy.213, s32[1024]{0:T(1024)S(1)} %get-tuple-element.203), kind=kCustom, calls=%fused_computation.5 | custom fusion | bytes 12583008 | tf_op jit(solution)/shard_map/gather | solution.py:86
  116.3 57.7 %all-to-all-done.2 = bf16[8,3,256,4,128]{2,4,3,1,0:T(8,128)(2,1)} async-done(((bf16[8,3,256,4,128]{2,4,3,1,0:T(8,128)(2,1)}), bf16[8,3,256,4,128]{2,4,3,1,0:T(8,128)(2,1)}, u32[]{:S(2)}, u32[]{:S(2)}) %all-to-all-start.2) | async-done | bytes 6291488 | tf_op jit(solution)/shard_map/all_to_all | solution.py:72
  173.9 103.8 %while.20 = (s32[]{:T(128)}, f32[8,3,4,256]{3,2,1,0:T(4,128)S(1)}, f32[8,3,4,256]{3,2,1,0:T(4,128)S(1)}, f32[8,3,256,4,128]{2,4,3,1,0:T(8,128)}, f32[8,3,4,256]{...) while((s32[]{:T(128)}, f32[8,3,4,256]{3,2,1,0:T(4,128)S(1)}, ...), condition=%wide.region_9.10_spmd, body=%wide.region_2.9_spmd.sunk | while | flops 619720704 | bytes 20795064 | solution.py:87
  176.3 2.5 multiply_reduce_fusion.8
  178.8 3.3 bitcast_dynamic-update-slice_fusion.5
  182.0 3.2 bitcast_dynamic-update-slice_fusion.4
  191.8 3.2 bitcast_dynamic-update-slice_fusion.5
  195.0 3.1 bitcast_dynamic-update-slice_fusion.4
  202.3 2.5 multiply_reduce_fusion.8
  204.8 3.2 bitcast_dynamic-update-slice_fusion.5
  208.0 3.1 bitcast_dynamic-update-slice_fusion.4
  215.2 2.5 multiply_reduce_fusion.8
  217.7 3.2 bitcast_dynamic-update-slice_fusion.5
  220.9 3.2 bitcast_dynamic-update-slice_fusion.4
  228.2 2.5 multiply_reduce_fusion.8
  230.7 3.2 bitcast_dynamic-update-slice_fusion.5
  233.9 3.1 bitcast_dynamic-update-slice_fusion.4
  241.2 2.5 multiply_reduce_fusion.8
  243.7 3.2 bitcast_dynamic-update-slice_fusion.5
  246.9 3.1 bitcast_dynamic-update-slice_fusion.4
  256.7 3.2 bitcast_dynamic-update-slice_fusion.5
  259.8 3.2 bitcast_dynamic-update-slice_fusion.4
  267.1 2.5 multiply_reduce_fusion.8
  269.7 3.2 bitcast_dynamic-update-slice_fusion.5
  272.9 3.1 bitcast_dynamic-update-slice_fusion.4
  277.8 7.6 %all_to_all.50 = f32[8,3,4,256]{3,2,1,0:T(4,128)S(1)} all-to-all(f32[8,3,4,256]{3,2,1,0:T(4,128)S(1)} %get-tuple-element.73), channel_id=1, replica_groups=mesh['seq'=8,'head'=4] {'seq'}, dimensions={0} | all-to-all | bytes 196608 | tf_op jit(solution)/shard_map/all_to_all | solution.py:90
  285.4 7.6 %all_to_all.51 = f32[8,3,4,256]{3,2,1,0:T(4,128)S(1)} all-to-all(f32[8,3,4,256]{3,2,1,0:T(4,128)S(1)} %get-tuple-element.77), channel_id=1, replica_groups=mesh['seq'=8,'head'=4] {'seq'}, dimensions={0} | all-to-all | bytes 196608 | tf_op jit(solution)/shard_map/all_to_all | solution.py:90
  293.0 6.8 %all-to-all-start.4 = ((f32[8,3,256,4,128]{2,4,3,1,0:T(8,128)}), f32[8,3,256,4,128]{2,4,3,1,0:T(8,128)}, u32[]{:S(2)}, u32[]{:S(2)}) async-start(f32[8,3,256,4,128]{2,4,3,1,0:T(8,128)} %get-tuple-element.75), calls=%async_computation.4 | async-start | bytes 25165824 | tf_op jit(solution)/shard_map/all_to_all | solution.py:90
  306.9 3.2 copy-done.3
  310.1 2.9 fusion.38
  314.4 13.2 %copy.230 = f32[24,256,4,128]{3,0,2,1:T(8,128)} copy(f32[24,256,4,128]{1,3,2,0:T(8,128)} %bitcast.134) | data formatting | bytes 25165824 | tf_op jit(solution)/shard_map/reshape | solution.py:111
  329.1 108.3 %all-to-all-done.4 = f32[8,3,256,4,128]{2,4,3,1,0:T(8,128)} async-done(((f32[8,3,256,4,128]{2,4,3,1,0:T(8,128)}), f32[8,3,256,4,128]{2,4,3,1,0:T(8,128)}, u32[]{:S(2)}, u32[]{:S(2)}) %all-to-all-start.4) | async-done | bytes 12582944 | tf_op jit(solution)/shard_map/all_to_all | solution.py:90
  437.4 12.9 %copy.231 = f32[24,256,4,128]{3,0,2,1:T(8,128)} copy(f32[24,256,4,128]{1,3,2,0:T(8,128)} %bitcast.33) | data formatting | bytes 25165824 | tf_op jit(solution)/shard_map/reshape | solution.py:112
  450.3 15.0 %fusion.33 = f32[8,256,4,128]{3,0,2,1:T(8,128)S(1)} fusion(f32[24,256,4,128]{3,0,2,1:T(8,128)} %copy.231, f32[24,256,4,128]{3,0,2,1:T(8,128)} %copy.230, f32[48,256,4]{0,2,1:T(4,128)S(1)} %copy.233, s32[48]{0:T(128)S(1)} %pad_add_fusion), kind=kOutput, calls=%fused_computation.49 | convolution fusion | flops 616563072 | bytes 29556928 | tf_op jit(solution)/shard_map/kb,kshd->bshd/dot_general | solution.py:129
  465.4 9.4 %fusion.44 = bf16[8,256,4,128]{3,1,2,0:T(8,128)(2,1)S(1)} fusion(f32[8,256,4,128]{3,0,2,1:T(8,128)S(1)} %fusion.33, f32[8,256,4]{1,2,0:T(4,128)S(1)} %copy.237, f32[8,256,4]{1,2,0:T(4,128)S(1)} %copy.229, f32[8,4,256,256]{2,3,1,0:T(8,128)} %copy-done.3, f32[8,4,256]{2,1,0:T(4,128)S(1)} %get-tuple-element.201, f32[8,4,256]{2,1,0:T(4,128)S(1)} %copy.210, ...), kind=kOutput, calls=%fused_computation.62 | convolution fusion | flops 549453824 | bytes 16973824 | tf_op jit(solution)/shard_map/vmap(hst,thd->shd)/dot_general | solution.py:47
  478.6 53.3 %all_to_all.52 = bf16[4,512,512]{2,1,0:T(8,128)(2,1)S(1)} all-to-all(bf16[4,512,512]{2,1,0:T(8,128)(2,1)} %convert_element_type.32), channel_id=1, replica_groups=mesh['seq'=8,'head'=4] {'head'}, dimensions={0} | all-to-all | bytes 4194304 | tf_op jit(solution)/shard_map/all_to_all | solution.py:137
  534.3 9.9 %convolution_convert_fusion = bf16[512,2048]{1,0:T(8,128)(2,1)} fusion(bf16[512,2048]{0,1:T(8,128)(2,1)} %bitcast.136, bf16[2048,2048]{1,0:T(8,128)(2,1)} %all-gather.2.cloned.1.call-done), kind=kOutput, calls=%fused_computation.68 | convolution fusion | flops 4296015872 | bytes 12582912 | tf_op jit(solution)/shard_map/dot_general | solution.py:138
  (126 shorter events, 59.6 us)
Async XLA Ops:
  6.5 107.9 %copy-start = (s32[64,16]{0,1:T(8,128)S(1)}, s32[64,16]{0,1:T(8,128)}, u32[]{:S(2)}) copy-start(s32[64,16]{0,1:T(8,128)} %param.11) | copy-start | bytes 12292
  7.9 10.3 %all-to-all-start = ((s32[1,8,3]{2,0,1:T(1,128)}), s32[1,8,3]{2,0,1:T(1,128)S(1)}, u32[]{:S(2)}, u32[]{:S(2)}) async-start(s32[1,8,3]{2,0,1:T(1,128)} %copy.216), calls=%async_computation | async-start | bytes 8192 | tf_op jit(solution)/shard_map/all_to_all | solution.py:65
  22.7 74.9 %all-to-all-start.1 = ((bf16[8,3,256,4,128]{4,2,3,1,0:T(8,128)(2,1)}), bf16[8,3,256,4,128]{4,2,3,1,0:T(8,128)(2,1)}, u32[]{:S(2)}, u32[]{:S(2)}) async-start(bf16[8,3,256,4,128]{4,2,3,1,0:T(8,128)(2,1)} %bitcast.131), calls=%async_computation.1 | async-start | bytes 12582912 | tf_op jit(solution)/shard_map/all_to_all | solution.py:71
  49.3 54.5 %copy-start.5 = (s32[1,8,3]{1,0,2:T(1,128)S(1)}, s32[1,8,3]{1,0,2:T(1,128)}, u32[]{:S(2)}) copy-start(s32[1,8,3]{1,0,2:T(1,128)} %param.13) | copy-start | bytes 292
  49.3 54.5 %copy-start.6 = (s32[1,8,3]{1,0,2:T(1,128)S(1)}, s32[1,8,3]{1,0,2:T(1,128)}, u32[]{:S(2)}) copy-start(s32[1,8,3]{1,0,2:T(1,128)} %param.12) | copy-start | bytes 292
  97.6 76.4 %all-to-all-start.2 = ((bf16[8,3,256,4,128]{2,4,3,1,0:T(8,128)(2,1)}), bf16[8,3,256,4,128]{2,4,3,1,0:T(8,128)(2,1)}, u32[]{:S(2)}, u32[]{:S(2)}) async-start(bf16[8,3,256,4,128]{2,4,3,1,0:T(8,128)(2,1)} %copy.225), calls=%async_computation.2 | async-start | bytes 12582912 | tf_op jit(solution)/shard_map/all_to_all | solution.py:72
  108.5 7.6 %copy-start.7 = (s32[1,8]{1,0:T(1,128)S(1)}, s32[1,8]{1,0:T(1,128)}, u32[]{:S(2)}) copy-start(s32[1,8]{1,0:T(1,128)} %param.14) | copy-start | bytes 100
  293.0 7.6 %copy-start.2 = (bf16[8,256,4,128]{3,2,1,0:T(4,128)(2,1)S(1)}, bf16[8,256,4,128]{3,2,1,0:T(4,128)(2,1)}, u32[]{:S(2)}) copy-start(bf16[8,256,4,128]{3,2,1,0:T(4,128)(2,1)} %reshape.322) | copy-start | bytes 6291460
  293.0 144.4 %all-to-all-start.4 = ((f32[8,3,256,4,128]{2,4,3,1,0:T(8,128)}), f32[8,3,256,4,128]{2,4,3,1,0:T(8,128)}, u32[]{:S(2)}, u32[]{:S(2)}) async-start(f32[8,3,256,4,128]{2,4,3,1,0:T(8,128)} %get-tuple-element.75), calls=%async_computation.4 | async-start | bytes 25165824 | tf_op jit(solution)/shard_map/all_to_all | solution.py:90
  299.8 234.5 %all-gather.2.cloned.1.call-start = ((), (), s32[]{:S(2)}) async-start(), calls=%async_computation.7 | async-start | bytes 10485760 | tf_op jit(solution)/shard_map/all_gather | solution.py:139
  306.9 3.2 copy-start.3
  450.3 15.0 %copy-start.4 = (bf16[8,256,4,128]{3,2,1,0:T(4,128)(2,1)S(1)}, bf16[8,256,4,128]{3,2,1,0:T(4,128)(2,1)}, u32[]{:S(2)}) copy-start(bf16[8,256,4,128]{3,2,1,0:T(4,128)(2,1)} %reshape.323) | copy-start | bytes 6291460
  534.3 9.9 %copy-start.1 = (s32[64,16]{0,1:T(8,128)S(1)}, s32[64,16]{0,1:T(8,128)}, u32[]{:S(2)}) copy-start(s32[64,16]{0,1:T(8,128)} %param.11) | copy-start | bytes 12292
Sparse Core Ops, SparseCore 0:
  302.2 150.7 all-gather.1
where the time goes:
time: 553 us; the launch traced here: 551 us
  waiting for transfers between devices  215 us (39%)
  matrix products  107 us (19%)
  local copies, waits for them, and re-layouts  85.2 us (15%)
  blocking collectives  68.5 us (12%)
  other arithmetic  39.5 us (7%)
  starting transfers between devices  22 us (4%)
  between operations  13.6 us (2%)
    all_to_all x1, waiting for transfers between devices, body(): lax.all_to_all(col_side, 'seq', split_axis=0, concat_axis=0, tiled=True)  108 us
    all_to_all x1, waiting for transfers between devices, body(): lax.all_to_all(sent_v, 'seq', split_axis=0, concat_axis=0, tiled=True)  57.7 us
    all_to_all x1, blocking collectives, body(): lax.all_to_all(attn, 'head', split_axis=0, concat_axis=1, tiled=True)  53.3 us
    all_to_all x1, waiting for transfers between devices, body(): lax.all_to_all(sent_q, 'seq', split_axis=0, concat_axis=0, tiled=True)  48.2 us
    dot_general x8, matrix products, pair_parts(): jnp.einsum('hst,shd->thd', pcol, v_a, preferred_element_type=jnp.float32)  25.6 us
    dot_general x8, matrix products, pair_parts(): jnp.einsum('hst,thd->shd', prow, v_b, preferred_element_type=jnp.float32)  25.1 us
    reduce_sum x9, other arithmetic, inverse_norms(): jnp.mean(wide * wide, axis=-1) + 1e-06  20.1 us
    dot_general x8, matrix products, pair_parts(): jnp.einsum('shd,thd->hst', q_a, q_b, preferred_element_type=jnp.float32)  19.9 us
  transfers between devices with their start and end apart: 5, of which 3 were waited for; matrix products, arithmetic and copies ran while one was open for 20% of the time, Pallas kernels for 0%

commit v1 on v0

--- a/solution.py
+++ b/solution.py
@@ -7,6 +7,28 @@
 HD = 128
 BLOCK = 256
 NEG = -1e30
+
+
+def cut_along(x, dim, size):
+    before, after = (x.shape[:dim], x.shape[dim + 1 :])
+    return jnp.moveaxis(x.reshape(*before, size, -1, *after), dim, 0)
+
+
+def in_order(blocks, dim):
+    blocks = jnp.moveaxis(blocks, 0, dim)
+    shape = blocks.shape
+    return blocks.reshape(*shape[:dim], shape[dim] * shape[dim + 1], *shape[dim + 2 :])
+
+
+def sent_to_each(array, axis, split_dim, concat_dim):
+    peers, here = (lax.axis_size(axis), lax.axis_index(axis))
+    pieces = cut_along(array, split_dim, peers)
+    finished = [pieces[here]]
+    for step in range(1, peers):
+        sent = pieces[(here + step) % peers]
+        finished.append(lax.ppermute(sent, axis, [(i, (i + step) % peers) for i in range(peers)]))
+    pieces = jnp.stack(finished)[(here - jnp.arange(peers)) % peers]
+    return in_order(pieces, concat_dim)
 
 
 def inverse_norms(block):
@@ -68,7 +90,7 @@
     sent_q = q_blocks[wanted].reshape(shards, slots, BLOCK, heads_here, HD)
     sent_v = v_blocks[wanted].reshape(shards, slots, BLOCK, heads_here, HD)
     got_q, got_v = (
-        lax.all_to_all(sent_q, "seq", split_axis=0, concat_axis=0, tiled=True),
+        sent_to_each(sent_q, "seq", 0, 0),
         lax.all_to_all(sent_v, "seq", split_axis=0, concat_axis=0, tiled=True),
     )
     row_index = pair_row.reshape(total_slots)

time: 553 us -> 562 us (1.016)
  waiting for transfers between devices: 215 us -> 184 us
  local copies, waits for them, and re-layouts: 85.2 us -> 108 us
  starting transfers between devices: 22 us -> 37.1 us
    ppermute x0 -> x7, waiting for transfers between devices: none -> 74.7 us  [sent_to_each(): lax.ppermute(sent, axis, [(i, (i + step) % peers) for i in range(peers)])]
    all_to_all x1, waiting for transfers between devices: 57.7 us -> 0.01 us  [body(): lax.all_to_all(sent_v, 'seq', split_axis=0, concat_axis=0, tiled=True)]
    all_to_all x1 -> x0, waiting for transfers between devices: 48.2 us -> none  [body(): lax.all_to_all(sent_q, 'seq', split_axis=0, concat_axis=0, tiled=True)]
    ppermute x0 -> x7, starting transfers between devices: none -> 21 us  [sent_to_each(): lax.ppermute(sent, axis, [(i, (i + step) % peers) for i in range(peers)])]
    unnamed x20 -> x24, local copies, waits for them, and re-layouts: 4.83 us -> 14.6 us
    gather x0 -> x1, local copies, waits for them, and re-layouts: none -> 6.72 us  [sent_to_each(): pieces = jnp.stack(finished)[(here - jnp.arange(peers)) % peers]]
  transfers between devices with their start and end apart: 5 -> 11, of which waited for: 3 -> 5; matrix products, arithmetic and copies ran while one was open for 20% -> 22% of each run, Pallas kernels for 0% -> 0%
where the time goes in v1:
time: 562 us; the launch traced here: 560 us
  waiting for transfers between devices  184 us (33%)
  local copies, waits for them, and re-layouts  108 us (19%)
  matrix products  107 us (19%)
  blocking collectives  70.4 us (13%)
  other arithmetic  39.5 us (7%)
  starting transfers between devices  37.1 us (7%)
  between operations  13.7 us (2%)
    all_to_all x1, waiting for transfers between devices, body(): lax.all_to_all(col_side, 'seq', split_axis=0, concat_axis=0, tiled=True)  108 us
    ppermute x7, waiting for transfers between devices, sent_to_each(): lax.ppermute(sent, axis, [(i, (i + step) % peers) for i in range(peers)])  74.7 us
    all_to_all x1, blocking collectives, body(): lax.all_to_all(attn, 'head', split_axis=0, concat_axis=1, tiled=True)  53.3 us
    dot_general x8, matrix products, pair_parts(): jnp.einsum('hst,shd->thd', pcol, v_a, preferred_element_type=jnp.float32)  25.6 us
    dot_general x8, matrix products, pair_parts(): jnp.einsum('hst,thd->shd', prow, v_b, preferred_element_type=jnp.float32)  25.1 us
    ppermute x7, starting transfers between devices, sent_to_each(): lax.ppermute(sent, axis, [(i, (i + step) % peers) for i in range(peers)])  21 us
    reduce_sum x9, other arithmetic, inverse_norms(): jnp.mean(wide * wide, axis=-1) + 1e-06  20.1 us
    dot_general x8, matrix products, pair_parts(): jnp.einsum('shd,thd->hst', q_a, q_b, preferred_element_type=jnp.float32)  19.9 us
  transfers between devices with their start and end apart: 11, of which 5 were waited for; matrix products, arithmetic and copies ran while one was open for 22% of the time, Pallas kernels for 0%

profile of v1, /device:TPU:2, one launch (start us, length us, event | category | flops | bytes accessed | tf_op | source)
XLA Modules:
  0.0 559.5 jit_solution(2798061254043671870)
XLA Ops:
  7.9 4.3 all-to-all-start
  13.1 4.0 reshape.383
  19.3 4.4 gather_fusion.5
  23.6 8.7 %copy.261 = bf16[8,3,256,4,128]{2,4,3,1,0:T(8,128)(2,1)} copy(bf16[8,3,256,4,128]{4,2,3,1,0:T(8,128)(2,1)} %bitcast.163) | data formatting | bytes 12582912 | tf_op jit(solution)/shard_map/reshape | solution.py:91
  32.3 4.8 all-to-all-start.1
  37.1 4.0 reshape.382
  41.1 3.5 copy.244
  44.7 5.9 %gather_fusion.3 = bf16[24,256,4,128]{3,1,2,0:T(8,128)(2,1)} fusion(bf16[8,256,4,128]{3,1,2,0:T(8,128)(2,1)} %copy.244, s32[1024]{0:T(1024)S(1)} %pad_clamp_fusion.1), kind=kCustom, calls=%fused_computation.3 | custom fusion | bytes 12583008 | tf_op jit(solution)/shard_map/gather | solution.py:90
  50.6 5.2 dynamic-slice_bitcast_fusion
  56.0 6.0 %gather_fusion.2 = bf16[24,256,4,128]{3,1,2,0:T(8,128)(2,1)} fusion(bf16[8,256,4,128]{3,1,2,0:T(8,128)(2,1)} %copy.244, s32[1024]{0:T(1024)S(1)} %get-tuple-element.225), kind=kCustom, calls=%fused_computation.2 | custom fusion | bytes 12583008 | tf_op jit(solution)/shard_map/gather | solution.py:107
  62.1 4.4 gather_fusion.6
  72.5 50.4 %collective-permute-done = bf16[1,3,256,4,128]{4,2,3,1,0:T(8,128)(2,1)} collective-permute-done((bf16[1,3,256,4,128]{4,2,3,1,0:T(8,128)(2,1)}, bf16[1,3,256,4,128]{4,2,3,1,0:T(8,128)(2,1)}, u32[]{:S(2)}, u32[]{:S(2)}) %collective-permute-start) | collective-permute-done | bytes 786464 | tf_op jit(solution)/shard_map/ppermute | solution.py:29
  127.2 14.2 %collective-permute-start.6 = (bf16[1,3,256,4,128]{4,2,3,1,0:T(8,128)(2,1)S(1)}, bf16[1,3,256,4,128]{4,2,3,1,0:T(8,128)(2,1)S(1)}, u32[]{:S(2)}, u32[]{:S(2)}) collective-permute-start(bf16[1,3,256,4,128]{4,2,3,1,0:T(8,128)(2,1)S(1)} %get-tuple-element.209), channel_id=1, source_target_pairs={{0,28},{4,0},{8,4},{12,8},{16,12},{20,16},{24,20},{28,24},{1,29},{... | collective-permute-start | bytes 2359304 | tf_op jit(solution)/shard_map/ppermute | solution.py:29
  146.6 10.6 %collective-permute-done.4 = bf16[1,3,256,4,128]{4,2,3,1,0:T(8,128)(2,1)S(1)} collective-permute-done((bf16[1,3,256,4,128]{4,2,3,1,0:T(8,128)(2,1)}, bf16[1,3,256,4,128]{4,2,3,1,0:T(8,128)(2,1)S(1)}, u32[]{:S(2)}, u32[]{:S(2)}) %collective-permute-start.4) | collective-permute-done | bytes 786464 | tf_op jit(solution)/shard_map/ppermute | solution.py:29
  159.3 13.4 %collective-permute-done.6 = bf16[1,3,256,4,128]{4,2,3,1,0:T(8,128)(2,1)S(1)} collective-permute-done((bf16[1,3,256,4,128]{4,2,3,1,0:T(8,128)(2,1)S(1)}, bf16[1,3,256,4,128]{4,2,3,1,0:T(8,128)(2,1)S(1)}, u32[]{:S(2)}, u32[]{:S(2)}) %collective-permute-start.6) | collective-permute-done | bytes 786464 | tf_op jit(solution)/shard_map/ppermute | solution.py:29
  173.6 6.7 %gather_fusion.4 = bf16[8,3,256,4,128]{4,2,3,1,0:T(8,128)(2,1)} fusion(bf16[8,3,256,4,128]{4,2,3,1,0:T(8,128)(2,1)} %bitcast.167, s32[1024]{0:T(1024)S(1)} %pad_clamp_fusion), kind=kCustom, calls=%fused_computation.4 | custom fusion | bytes 12582944 | tf_op jit(solution)/shard_map/gather | solution.py:30
  180.3 103.7 %while.20 = (s32[]{:T(128)}, f32[8,3,4,256]{3,2,1,0:T(4,128)S(1)}, f32[8,3,4,256]{3,2,1,0:T(4,128)S(1)}, f32[8,3,256,4,128]{2,4,3,1,0:T(8,128)}, f32[8,3,4,256]{...) while((s32[]{:T(128)}, f32[8,3,4,256]{3,2,1,0:T(4,128)S(1)}, ...), condition=%wide.region_9.10_spmd, body=%wide.region_2.9_spmd.sunk | while | flops 619720704 | bytes 20795064 | solution.py:109
  182.7 2.5 multiply_reduce_fusion.8
  185.2 3.2 bitcast_dynamic-update-slice_fusion.12
  188.4 3.1 bitcast_dynamic-update-slice_fusion.11
  198.2 3.2 bitcast_dynamic-update-slice_fusion.12
  201.3 3.1 bitcast_dynamic-update-slice_fusion.11
  211.1 3.2 bitcast_dynamic-update-slice_fusion.12
  214.2 3.1 bitcast_dynamic-update-slice_fusion.11
  221.5 2.5 multiply_reduce_fusion.8
  224.0 3.2 bitcast_dynamic-update-slice_fusion.12
  227.2 3.1 bitcast_dynamic-update-slice_fusion.11
  237.0 3.2 bitcast_dynamic-update-slice_fusion.12
  240.2 3.1 bitcast_dynamic-update-slice_fusion.11
  249.9 3.2 bitcast_dynamic-update-slice_fusion.12
  253.1 3.2 bitcast_dynamic-update-slice_fusion.11
  263.0 3.2 bitcast_dynamic-update-slice_fusion.12
  266.2 3.1 bitcast_dynamic-update-slice_fusion.11
  273.5 2.5 multiply_reduce_fusion.8
  276.0 3.2 bitcast_dynamic-update-slice_fusion.12
  279.2 3.1 bitcast_dynamic-update-slice_fusion.11
  284.1 9.6 %all_to_all.45 = f32[8,3,4,256]{3,2,1,0:T(4,128)S(1)} all-to-all(f32[8,3,4,256]{3,2,1,0:T(4,128)S(1)} %get-tuple-element.73), channel_id=1, replica_groups=mesh['seq'=8,'head'=4] {'seq'}, dimensions={0} | all-to-all | bytes 196608 | tf_op jit(solution)/shard_map/all_to_all | solution.py:112
  293.7 7.6 %all_to_all.46 = f32[8,3,4,256]{3,2,1,0:T(4,128)S(1)} all-to-all(f32[8,3,4,256]{3,2,1,0:T(4,128)S(1)} %get-tuple-element.77), channel_id=1, replica_groups=mesh['seq'=8,'head'=4] {'seq'}, dimensions={0} | all-to-all | bytes 196608 | tf_op jit(solution)/shard_map/all_to_all | solution.py:112
  301.2 7.1 %all-to-all-start.3 = ((f32[8,3,256,4,128]{2,4,3,1,0:T(8,128)}), f32[8,3,256,4,128]{2,4,3,1,0:T(8,128)}, u32[]{:S(2)}, u32[]{:S(2)}) async-start(f32[8,3,256,4,128]{2,4,3,1,0:T(8,128)} %get-tuple-element.75), calls=%async_computation.3 | async-start | bytes 25165824 | tf_op jit(solution)/shard_map/all_to_all | solution.py:112
  315.4 3.2 copy-done.3
  318.6 2.9 fusion.38
  322.9 13.2 %copy.266 = f32[24,256,4,128]{3,0,2,1:T(8,128)} copy(f32[24,256,4,128]{1,3,2,0:T(8,128)} %bitcast.165) | data formatting | bytes 25165824 | tf_op jit(solution)/shard_map/reshape | solution.py:133
  337.6 108.3 %all-to-all-done.3 = f32[8,3,256,4,128]{2,4,3,1,0:T(8,128)} async-done(((f32[8,3,256,4,128]{2,4,3,1,0:T(8,128)}), f32[8,3,256,4,128]{2,4,3,1,0:T(8,128)}, u32[]{:S(2)}, u32[]{:S(2)}) %all-to-all-start.3) | async-done | bytes 12582944 | tf_op jit(solution)/shard_map/all_to_all | solution.py:112
  445.9 12.9 %copy.267 = f32[24,256,4,128]{3,0,2,1:T(8,128)} copy(f32[24,256,4,128]{1,3,2,0:T(8,128)} %bitcast.49) | data formatting | bytes 25165824 | tf_op jit(solution)/shard_map/reshape | solution.py:134
  458.8 15.0 %fusion.33 = f32[8,256,4,128]{3,0,2,1:T(8,128)S(1)} fusion(f32[24,256,4,128]{3,0,2,1:T(8,128)} %copy.267, f32[24,256,4,128]{3,0,2,1:T(8,128)} %copy.266, f32[48,256,4]{0,2,1:T(4,128)S(1)} %copy.269, s32[48]{0:T(128)S(1)} %pad_add_fusion), kind=kOutput, calls=%fused_computation.50 | convolution fusion | flops 616563072 | bytes 29556928 | tf_op jit(solution)/shard_map/kb,kshd->bshd/dot_general | solution.py:151
  473.9 9.4 %fusion.44 = bf16[8,256,4,128]{3,1,2,0:T(8,128)(2,1)S(1)} fusion(f32[8,256,4,128]{3,0,2,1:T(8,128)S(1)} %fusion.33, f32[8,256,4]{1,2,0:T(4,128)S(1)} %copy.273, f32[8,256,4]{1,2,0:T(4,128)S(1)} %copy.265, f32[8,4,256,256]{2,3,1,0:T(8,128)} %copy-done.3, f32[8,4,256]{2,1,0:T(4,128)S(1)} %get-tuple-element.221, f32[8,4,256]{2,1,0:T(4,128)S(1)} %copy.246, ...), kind=kOutput, calls=%fused_computation.63 | convolution fusion | flops 549453824 | bytes 16973824 | tf_op jit(solution)/shard_map/vmap(hst,thd->shd)/dot_general | solution.py:69
  487.1 53.3 %all_to_all.47 = bf16[4,512,512]{2,1,0:T(8,128)(2,1)S(1)} all-to-all(bf16[4,512,512]{2,1,0:T(8,128)(2,1)} %convert_element_type.32), channel_id=1, replica_groups=mesh['seq'=8,'head'=4] {'head'}, dimensions={0} | all-to-all | bytes 4194304 | tf_op jit(solution)/shard_map/all_to_all | solution.py:159
  542.8 9.9 %convolution_convert_fusion = bf16[512,2048]{1,0:T(8,128)(2,1)} fusion(bf16[512,2048]{0,1:T(8,128)(2,1)} %bitcast.168, bf16[2048,2048]{1,0:T(8,128)(2,1)} %all-gather.2.cloned.1.call-done), kind=kOutput, calls=%fused_computation.69 | convolution fusion | flops 4296015872 | bytes 12582912 | tf_op jit(solution)/shard_map/dot_general | solution.py:160
  (146 shorter events, 84.6 us)
Async XLA Ops:
  6.5 49.5 %copy-start = (s32[64,16]{0,1:T(8,128)S(1)}, s32[64,16]{0,1:T(8,128)}, u32[]{:S(2)}) copy-start(s32[64,16]{0,1:T(8,128)} %param.11) | copy-start | bytes 12292
  7.9 11.3 %all-to-all-start = ((s32[1,8,3]{2,0,1:T(1,128)}), s32[1,8,3]{2,0,1:T(1,128)S(1)}, u32[]{:S(2)}, u32[]{:S(2)}) async-start(s32[1,8,3]{2,0,1:T(1,128)} %copy.252), calls=%async_computation | async-start | bytes 8192 | tf_op jit(solution)/shard_map/all_to_all | solution.py:87
  32.3 148.1 %all-to-all-start.1 = ((bf16[8,3,256,4,128]{2,4,3,1,0:T(8,128)(2,1)}), bf16[8,3,256,4,128]{2,4,3,1,0:T(8,128)(2,1)}, u32[]{:S(2)}, u32[]{:S(2)}) async-start(bf16[8,3,256,4,128]{2,4,3,1,0:T(8,128)(2,1)} %copy.261), calls=%async_computation.1 | async-start | bytes 12582912 | tf_op jit(solution)/shard_map/all_to_all | solution.py:94
  37.1 7.5 %copy-start.5 = (s32[1,8,3]{1,0,2:T(1,128)S(1)}, s32[1,8,3]{1,0,2:T(1,128)}, u32[]{:S(2)}) copy-start(s32[1,8,3]{1,0,2:T(1,128)} %param.12) | copy-start | bytes 292
  55.8 67.0 %collective-permute-start = (bf16[1,3,256,4,128]{4,2,3,1,0:T(8,128)(2,1)}, bf16[1,3,256,4,128]{4,2,3,1,0:T(8,128)(2,1)}, u32[]{:S(2)}, u32[]{:S(2)}) collective-permute-start(bf16[1,3,256,4,128]{4,2,3,1,0:T(8,128)(2,1)} %get-tuple-element.215), channel_id=1, source_target_pairs={{0,4},{4,8},{8,12},{12,16},{16,20},{20,24},{24,28},{28,0},{1,5},{5... | collective-permute-start | bytes 2359304 | tf_op jit(solution)/shard_map/ppermute | solution.py:29
  62.1 6.6 %copy-start.6 = (s32[1,8]{1,0:T(1,128)S(1)}, s32[1,8]{1,0:T(1,128)}, u32[]{:S(2)}) copy-start(s32[1,8]{1,0:T(1,128)} %param.14) | copy-start | bytes 100
  67.2 60.0 %collective-permute-start.1 = (bf16[1,3,256,4,128]{4,2,3,1,0:T(8,128)(2,1)}, bf16[1,3,256,4,128]{4,2,3,1,0:T(8,128)(2,1)}, u32[]{:S(2)}, u32[]{:S(2)}) collective-permute-start(bf16[1,3,256,4,128]{4,2,3,1,0:T(8,128)(2,1)} %get-tuple-element.214), channel_id=1, source_target_pairs={{0,8},{4,12},{8,16},{12,20},{16,24},{20,28},{24,0},{28,4},{1,9},{5... | collective-permute-start | bytes 2359304 | tf_op jit(solution)/shard_map/ppermute | solution.py:29
  68.8 74.7 %collective-permute-start.2 = (bf16[1,3,256,4,128]{4,2,3,1,0:T(8,128)(2,1)}, bf16[1,3,256,4,128]{4,2,3,1,0:T(8,128)(2,1)}, u32[]{:S(2)}, u32[]{:S(2)}) collective-permute-start(bf16[1,3,256,4,128]{4,2,3,1,0:T(8,128)(2,1)} %get-tuple-element.213), channel_id=1, source_target_pairs={{0,12},{4,16},{8,20},{12,24},{16,28},{20,0},{24,4},{28,8},{1,13},{... | collective-permute-start | bytes 2359304 | tf_op jit(solution)/shard_map/ppermute | solution.py:29
  69.9 75.7 %collective-permute-start.3 = (bf16[1,3,256,4,128]{4,2,3,1,0:T(8,128)(2,1)}, bf16[1,3,256,4,128]{4,2,3,1,0:T(8,128)(2,1)S(1)}, u32[]{:S(2)}, u32[]{:S(2)}) collective-permute-start(bf16[1,3,256,4,128]{4,2,3,1,0:T(8,128)(2,1)} %get-tuple-element.212), channel_id=1, source_target_pairs={{0,16},{4,20},{8,24},{12,28},{16,0},{20,4},{24,8},{28,12},{1,17},{... | collective-permute-start | bytes 2359304 | tf_op jit(solution)/shard_map/ppermute | solution.py:29
  71.5 85.7 %collective-permute-start.4 = (bf16[1,3,256,4,128]{4,2,3,1,0:T(8,128)(2,1)}, bf16[1,3,256,4,128]{4,2,3,1,0:T(8,128)(2,1)S(1)}, u32[]{:S(2)}, u32[]{:S(2)}) collective-permute-start(bf16[1,3,256,4,128]{4,2,3,1,0:T(8,128)(2,1)} %get-tuple-element.211), channel_id=1, source_target_pairs={{0,20},{4,24},{8,28},{12,0},{16,4},{20,8},{24,12},{28,16},{1,21},{... | collective-permute-start | bytes 2359304 | tf_op jit(solution)/shard_map/ppermute | solution.py:29
  122.8 35.5 %collective-permute-start.5 = (bf16[1,3,256,4,128]{4,2,3,1,0:T(8,128)(2,1)}, bf16[1,3,256,4,128]{4,2,3,1,0:T(8,128)(2,1)S(1)}, u32[]{:S(2)}, u32[]{:S(2)}) collective-permute-start(bf16[1,3,256,4,128]{4,2,3,1,0:T(8,128)(2,1)} %get-tuple-element.210), channel_id=1, source_target_pairs={{0,24},{4,28},{8,0},{12,4},{16,8},{20,12},{24,16},{28,20},{1,25},{... | collective-permute-start | bytes 2359304 | tf_op jit(solution)/shard_map/ppermute | solution.py:29
  127.2 45.5 %collective-permute-start.6 = (bf16[1,3,256,4,128]{4,2,3,1,0:T(8,128)(2,1)S(1)}, bf16[1,3,256,4,128]{4,2,3,1,0:T(8,128)(2,1)S(1)}, u32[]{:S(2)}, u32[]{:S(2)}) collective-permute-start(bf16[1,3,256,4,128]{4,2,3,1,0:T(8,128)(2,1)S(1)} %get-tuple-element.209), channel_id=1, source_target_pairs={{0,28},{4,0},{8,4},{12,8},{16,12},{20,16},{24,20},{28,24},{1,29},{... | collective-permute-start | bytes 2359304 | tf_op jit(solution)/shard_map/ppermute | solution.py:29
  301.2 7.9 %copy-start.2 = (bf16[8,256,4,128]{3,2,1,0:T(4,128)(2,1)S(1)}, bf16[8,256,4,128]{3,2,1,0:T(4,128)(2,1)}, u32[]{:S(2)}) copy-start(bf16[8,256,4,128]{3,2,1,0:T(4,128)(2,1)} %reshape.382) | copy-start | bytes 6291460
  301.2 144.7 %all-to-all-start.3 = ((f32[8,3,256,4,128]{2,4,3,1,0:T(8,128)}), f32[8,3,256,4,128]{2,4,3,1,0:T(8,128)}, u32[]{:S(2)}, u32[]{:S(2)}) async-start(f32[8,3,256,4,128]{2,4,3,1,0:T(8,128)} %get-tuple-element.75), calls=%async_computation.3 | async-start | bytes 25165824 | tf_op jit(solution)/shard_map/all_to_all | solution.py:112
  308.3 234.5 %all-gather.2.cloned.1.call-start = ((), (), s32[]{:S(2)}) async-start(), calls=%async_computation.6 | async-start | bytes 10485760 | tf_op jit(solution)/shard_map/all_gather | solution.py:161
  315.4 3.2 copy-start.3
  458.8 15.0 %copy-start.4 = (bf16[8,256,4,128]{3,2,1,0:T(4,128)(2,1)S(1)}, bf16[8,256,4,128]{3,2,1,0:T(4,128)(2,1)}, u32[]{:S(2)}) copy-start(bf16[8,256,4,128]{3,2,1,0:T(4,128)(2,1)} %reshape.383) | copy-start | bytes 6291460
  542.8 9.9 %copy-start.1 = (s32[64,16]{0,1:T(8,128)S(1)}, s32[64,16]{0,1:T(8,128)}, u32[]{:S(2)}) copy-start(s32[64,16]{0,1:T(8,128)} %param.11) | copy-start | bytes 12292
Sparse Core Ops, SparseCore 0:
  310.7 150.7 all-gather.1
